TPU v7x, 512 devices: a whole 4x8x8 slice. The times are simulated.
512 devices in a mesh: param: 128 (over y, x_lo, z), ex: 4 (over x_hi, core).
Axes of the slice: x: 4 (x_hi: 2, x_lo: 2; x = x_hi * 2 + x_lo), y: 8, z: 8, core: 2. Of those that a mesh axis runs over, the one named last changes fastest.
Arguments:
- inputs: bfloat16 [4, 256, 8192], P('ex', 'param'), may hold values from -6 to 6
- cotangents: bfloat16 [4, 256, 16384], P('ex', None, 'param'), may hold values from -0.375 to 0.375
- sign_flips: bfloat16 [16384, 8192], P('param'), may hold values from -1 to 1, as said below
- sample_rows: int32 [8192], replicated, may hold values from 0 to 16383
- sample_columns: int32 [8192], replicated, may hold values from 0 to 8191
Outputs:
- sketch: float32 [4, 8192], P('ex', 'param')
Inputs may be any that keep to these rules, and one draw needn't show every extreme that they name: `sign_flips`: every entry is +1 or -1.
All inputs are finite; a program needn't handle non-finite values.
Results may differ from a plain program's by a relative error of at most 0.0003.
Values may be sent and summed in bfloat16 or wider, within the bound.
No kernel may reach another device: no remote copies, remote signals or barrier semaphores. Data moves between devices by JAX's collectives and lax.ppermute only.
A program may use at most 64 MiB of HBM per device.

v0:
```python
import functools, math
import jax, jax.numpy as jnp
from jax import lax
from jax.sharding import PartitionSpec as P
from jax.experimental import pallas as pl
from jax.experimental.pallas import tpu as pltpu

LANES = 128
STEP = 8 * LANES


def hadamard_table(order):
    p = lax.iota(jnp.int32, order)
    odd = lax.population_count(p[:, None] & p[None, :]) & 1
    return (1 - 2 * odd).astype(jnp.bfloat16)


def split(v):
    hi = v.astype(jnp.bfloat16)
    return hi, (v - hi.astype(jnp.float32)).astype(jnp.bfloat16)


def butterfly(parts):
    parts, stride = list(parts), 1
    while stride < len(parts):
        for i in range(len(parts)):
            if not i & stride:
                a, b = parts[i], parts[i | stride]
                parts[i], parts[i | stride] = a + b, a - b
        stride *= 2
    return parts


def kernel(norm, index, core, grads, tokens, own, near, far, near_half, far_half, table, rows_sign, out, *scratch):
    block, even, odd, own_v, near_v, far_v, near_half_v, far_half_v, here, later, arrived, listed = scratch
    rows = grads.shape[1]
    me = core[0]
    span = tokens.shape[1]
    group = here.shape[0]
    groups = index.shape[0] // group
    sources = (own.at[:, pl.ds(pl.multiple_of(core[1] * span, span), span)], near, far, near_half, far_half)
    signs = (own_v, near_v, far_v, near_half_v, far_half_v)
    copies = [pltpu.make_async_copy(a, b, arrived.at[i]) for i, (a, b) in enumerate(zip(sources, signs))]

    def fetch(i, part, places):
        start = pl.multiple_of(i * group, group)
        return pltpu.make_async_copy(index.at[pl.ds(start, group)], places, listed.at[part])

    for copy in copies:
        copy.start()
    fetch(0, 0, here).start()
    fetch(1, 1, later).start()

    def chunk(signs, start, slot, half):
        cols = pl.ds(pl.multiple_of(half * STEP, STEP), STEP)
        g = jnp.dot(grads[slot], tokens[:, cols], preferred_element_type=jnp.float32)
        f = g * signs[:, pl.ds(pl.multiple_of(start, STEP), STEP)].astype(jnp.float32)
        r = jnp.dot(rows_sign[...], jnp.concatenate(split(f), 0), preferred_element_type=jnp.float32)
        for t in range(rows // 8):
            parts = butterfly([r[8 * t : 8 * t + 8, LANES * u : LANES * u + LANES] for u in range(8)])
            for u in range(8):
                base = ((slot * 2 + half) * 8 + u) * rows + 8 * t
                block[pl.ds(pl.multiple_of(base, 8), 8), :] = parts[u]

    for i, slot in enumerate((0, 2 - me, 1 + me)):
        copies[i].wait()

        @pl.loop(0, 2)
        def _(half):
            chunk(signs[i], half * STEP, slot, half)
    for i, half in ((3, me), (4, 1 - me)):
        copies[i].wait()
        chunk(signs[i], 0, 3, half)

    @pl.loop(0, rows // 8)
    def _(t):
        for u in range(8):
            at = [pl.ds(pl.multiple_of((8 * c + u) * rows + 8 * t, 8), 8) for c in range(8)]
            for w, v in zip(at, butterfly([block[w, :] for w in at])):
                block[w, :] = v

    shape = (LANES, LANES)
    eye = lax.broadcasted_iota(jnp.int32, shape, 0) == lax.broadcasted_iota(jnp.int32, shape, 1)

    def gather(places, row, picked):
        for s in range(LANES):
            picked[pl.ds(s, 1), :] = block[pl.ds(places[row, s], 1), :]

    def select(b, picked):
        m = table[b]
        z = jnp.dot(
            jnp.concatenate(split(picked[...]), 1), jnp.concatenate([m, m], 0), preferred_element_type=jnp.float32
        )
        out[pl.ds(b, 1), :] = jnp.sum(jnp.where(eye, z, 0.0), axis=0, keepdims=True) * norm

    buffers = (even, odd)

    @pl.loop(0, groups // 2)
    def _(i):
        for part, places in enumerate((here, later)):
            g = 2 * i + part
            fetch(g, part, places).wait()
            for row in range(group):
                gather(places, row, buffers[row % 2])
                if row:
                    select(g * group + row - 1, buffers[1 - row % 2])

            @pl.when(i < groups // 2 - 1)
            def _():
                fetch(g + 2, part, places).start()

            select(g * group + group - 1, buffers[1 - group % 2])


def local_call(norm, index, core, grads, tokens, own, near, far, near_half, far_half, table):
    rows = grads.shape[1]
    h = hadamard_table(rows)
    smem, vmem, held = (pl.BlockSpec(memory_space=m) for m in (pltpu.SMEM, pltpu.VMEM, pl.ANY))
    places = pltpu.SMEM((8, LANES), jnp.int32)
    signs = (own, near, far, near_half, far_half)
    widths = (near.shape[1],) * 3 + (near_half.shape[1],) * 2
    return pl.pallas_call(
        functools.partial(kernel, norm),
        out_shape=jax.ShapeDtypeStruct(index.shape, jnp.float32),
        in_specs=[vmem, smem, vmem, vmem] + [held] * 5 + [vmem, vmem],
        out_specs=vmem,
        scratch_shapes=[
            pltpu.VMEM((grads.shape[0] * rows * tokens.shape[1] // LANES, LANES), jnp.float32),
            pltpu.VMEM((LANES, LANES), jnp.float32),
            pltpu.VMEM((LANES, LANES), jnp.float32),
            *(pltpu.VMEM((rows, w), own.dtype) for w in widths),
            places,
            places,
            pltpu.SemaphoreType.DMA((len(signs),)),
            pltpu.SemaphoreType.DMA((2,)),
        ],
        compiler_params=pltpu.CompilerParams(vmem_limit_bytes=40 << 20),
    )(index, core, grads, tokens, *signs, table, jnp.concatenate([h, h], 1))


def odd_bits(v):
    return lax.population_count(v) & 1


def shards(inputs, cotangents, sign_flips, sample_rows, sample_columns):
    zs, xs, ys, cores = 8, 2, 8, 2
    own = lax.axis_index("param")
    ex = lax.axis_index("ex")
    core = ex % cores
    parts = lax.axis_size("param")
    examples = lax.axis_size("ex")
    rows, width = sign_flips.shape
    norm = 1.0 / math.sqrt(parts * rows * width)
    shift = (0, 1, zs, zs + 1)
    place = (own >> 3 & 1) * 2 + (own & 1)
    span = width // 4

    def columns(start_place, start, size):
        return lax.dynamic_slice_in_dim(sign_flips, start_place * span + start, size, 1)

    def send(value, slot_of_core):
        pairs = [
            (p * examples + e, (p ^ shift[slot_of_core[e % cores]]) * examples + e)
            for p in range(ys * xs * zs) for e in range(examples)
        ]
        return lax.ppermute(value, ("param", "ex"), pairs)

    swap = [(e, e ^ 1) for e in range(examples)]

    near = send(columns(place ^ (2 - core), 0, span), (2, 1))
    near_half = send(columns(place ^ 3, core * (span // 2), span // 2), (3, 3))
    tokens = inputs[0].reshape(-1, xs, 2, span).transpose(1, 2, 0, 3)
    tokens = jnp.broadcast_to(tokens[None, :, None], (ys, xs, zs // 2, 2) + tokens.shape[2:])
    tokens = lax.all_to_all(tokens.reshape(parts, -1, span), "param", 0, 0, tiled=True)
    tokens = tokens.reshape(-1, span)
    far = lax.ppermute(near, "ex", swap)
    far_half = lax.ppermute(near_half, "ex", swap)
    grad = cotangents[0].T
    grads = [grad]
    for s in (1, 2, 3):
        grads.append(send(grad, (s, s)))
    grads = jnp.stack(grads)

    owner, row = sample_rows // rows, sample_rows % rows
    slot = (owner >> 3 & 1) * 2 + (owner & 1)
    index = (slot * (span // LANES) + sample_columns // LANES % (span // LANES)) * rows + row
    index = index.reshape(-1, LANES)
    odd = odd_bits(owner & own) + odd_bits(sample_columns // span & place)
    lane = lax.iota(jnp.int32, LANES)
    odd = odd.reshape(-1, 1, LANES) + odd_bits(lane[None, :, None] & (sample_columns % LANES).reshape(-1, 1, LANES))
    table = (1 - 2 * (odd & 1)).astype(jnp.bfloat16)

    picked = local_call(
        norm, index, jnp.stack([core, place]), grads, tokens, sign_flips, near, far, near_half, far_half, table
    )
    return lax.all_to_all(picked.reshape(parts, 1, -1), "param", 0, 0, tiled=True).sum(0)


def solution(mesh):
    return jax.shard_map(
        shards,
        mesh=mesh,
        in_specs=(P("ex", "param", None), P("ex", None, "param"), P("param", None), P(), P()),
        out_specs=P("ex", "param"),
        check_vma=False,
    )
```

profile of v0, /device:TPU:1, one launch (start us, length us, event | category | flops | bytes accessed | tf_op | source)
XLA Modules:
  0.0 103.4 jit_solution(1184722362080986270)
XLA Ops:
  0.0 0.8 reshape_squeeze.3
  0.8 0.0 copy-start.1
  0.8 2.0 %broadcast_in_dim.2 = bf16[8,2,4,2,2,2048]{5,4,3,2,1,0:T(2,128)(2,1)} broadcast(bf16[2,2,2,2048]{3,2,1,0:T(2,128)(2,1)S(1)} %copy.11), dimensions={1,3,4,5} | broadcast | bytes 1081344 | tf_op jit(solution)/shard_map/broadcast_in_dim | solution.py:173
  2.9 0.0 copy-start.2
  2.9 0.0 copy-start.3
  2.9 19.9 %all-to-all-start = ((bf16[128,2,2048]{2,1,0:T(2,128)(2,1)}), bf16[128,2,2048]{2,1,0:T(2,128)(2,1)}, u32[]{:S(2)}, u32[]{:S(2)}) async-start(bf16[128,2,2048]{2,1,0:T(2,128)(2,1)} %bitcast.11), calls=%async_computation | async-start | bytes 2097152 | tf_op jit(solution)/shard_map/all_to_all | solution.py:174
  22.8 1.1 %constant_dynamic-slice_fusion.1 = bf16[128,2048]{1,0:T(8,128)(2,1)S(1)} fusion(bf16[128,8192]{1,0:T(8,128)(2,1)} %own.1, s32[]{:T(128)S(6)} %select_n.43), kind=kLoop, calls=%fused_computation.40 | loop fusion | bytes 1048580 | tf_op jit(solution)/shard_map/dynamic_slice | solution.py:159
  23.9 2.4 %collective-permute-start.3 = (bf16[128,2048]{1,0:T(8,128)(2,1)S(1)}, bf16[128,2048]{1,0:T(8,128)(2,1)}, u32[]{:S(2)}, u32[]{:S(2)}) collective-permute-start(bf16[128,2048]{1,0:T(8,128)(2,1)S(1)} %constant_dynamic-slice_fusion.1), channel_id=1, source_target_pairs={{0,32},{1,5},{2,34},{3,7},{4,36},{5,1},{6,38},{7,3},{8,40},{9,13},... | collective-permute-start | bytes 1572872 | tf_op jit(solution)/shard_map/ppermute | solution.py:166
  26.3 0.0 copy-done.1
  26.3 0.1 copy.10
  26.5 3.1 %collective-permute-start.2 = (bf16[128,256]{1,0:T(8,128)(2,1)S(1)}, bf16[128,256]{1,0:T(8,128)(2,1)S(1)}, u32[]{:S(2)}, u32[]{:S(2)}) collective-permute-start(bf16[128,256]{1,0:T(8,128)(2,1)S(1)} %bitcast.21), channel_id=1, source_target_pairs={{0,36},{1,37},{2,38},{3,39},{4,32},{5,33},{6,34},{7,35},{8,44},{9,... | collective-permute-start | bytes 196616 | tf_op jit(solution)/shard_map/ppermute | solution.py:166
  29.6 2.9 %collective-permute-start.1 = (bf16[128,256]{1,0:T(8,128)(2,1)S(1)}, bf16[128,256]{1,0:T(8,128)(2,1)S(1)}, u32[]{:S(2)}, u32[]{:S(2)}) collective-permute-start(bf16[128,256]{1,0:T(8,128)(2,1)S(1)} %bitcast.22), channel_id=1, source_target_pairs={{0,32},{1,33},{2,34},{3,35},{4,36},{5,37},{6,38},{7,39},{8,40},{9,... | collective-permute-start | bytes 196616 | tf_op jit(solution)/shard_map/ppermute | solution.py:166
  32.4 2.4 %collective-permute-start = (bf16[128,256]{1,0:T(8,128)(2,1)S(1)}, bf16[128,256]{1,0:T(8,128)(2,1)S(1)}, u32[]{:S(2)}, u32[]{:S(2)}) collective-permute-start(bf16[128,256]{1,0:T(8,128)(2,1)S(1)} %bitcast.23), channel_id=1, source_target_pairs={{0,4},{1,5},{2,6},{3,7},{4,0},{5,1},{6,2},{7,3},{8,12},{9,13},{10,... | collective-permute-start | bytes 196616 | tf_op jit(solution)/shard_map/ppermute | solution.py:166
  34.9 1.0 constant_dynamic-slice_fusion
  35.8 3.1 %collective-permute-start.5 = (bf16[128,1024]{1,0:T(8,128)(2,1)S(1)}, bf16[128,1024]{1,0:T(8,128)(2,1)}, u32[]{:S(2)}, u32[]{:S(2)}) collective-permute-start(bf16[128,1024]{1,0:T(8,128)(2,1)S(1)} %constant_dynamic-slice_fusion), channel_id=1, source_target_pairs={{0,36},{1,37},{2,38},{3,39},{4,32},{5,33},{6,34},{7,35},{8,44},{9,... | collective-permute-start | bytes 786440 | tf_op jit(solution)/shard_map/ppermute | solution.py:166
  38.9 0.0 copy-done.2
  39.0 0.0 copy-done.3
  39.0 0.1 fusion.10
  39.1 17.2 %collective-permute-done.3.near = bf16[128,2048]{1,0:T(8,128)(2,1)} collective-permute-done((bf16[128,2048]{1,0:T(8,128)(2,1)S(1)}, bf16[128,2048]{1,0:T(8,128)(2,1)}, u32[]{:S(2)}, u32[]{:S(2)}) %collective-permute-start.3) | collective-permute-done | bytes 524320 | tf_op jit(solution)/shard_map/ppermute | solution.py:166
  56.3 1.9 %collective-permute-start.4 = (bf16[128,2048]{1,0:T(8,128)(2,1)}, bf16[128,2048]{1,0:T(8,128)(2,1)}, u32[]{:S(2)}, u32[]{:S(2)}) collective-permute-start(bf16[128,2048]{1,0:T(8,128)(2,1)} %collective-permute-done.3.near), channel_id=1, source_target_pairs={{0,1},{1,0},{2,3},{3,2},{4,5},{5,4},{6,7},{7,6},{8,9},{9,8},{10,11... | collective-permute-start | bytes 1572872 | tf_op jit(solution)/shard_map/ppermute | solution.py:176
  58.2 1.3 %subtract_convert_fusion.table = bf16[64,128,128]{2,1,0:T(8,128)(2,1)S(1)} fusion(s32[64,128]{1,0:T(8,128)S(1)} %get-tuple-element.7, s32[64,128]{1,0:T(8,128)S(1)} %get-tuple-element.5), kind=kLoop, calls=%fused_computation | loop fusion | flops 8388608 | bytes 2162688 | tf_op jit(solution)/shard_map/convert_element_type | solution.py:191
  59.5 1.8 %collective-permute-done.5.near_half = bf16[128,1024]{1,0:T(8,128)(2,1)} collective-permute-done((bf16[128,1024]{1,0:T(8,128)(2,1)S(1)}, bf16[128,1024]{1,0:T(8,128)(2,1)}, u32[]{:S(2)}, u32[]{:S(2)}) %collective-permute-start.5) | collective-permute-done | bytes 262176 | tf_op jit(solution)/shard_map/ppermute | solution.py:166
  61.4 1.9 %collective-permute-start.6 = (bf16[128,1024]{1,0:T(8,128)(2,1)}, bf16[128,1024]{1,0:T(8,128)(2,1)}, u32[]{:S(2)}, u32[]{:S(2)}) collective-permute-start(bf16[128,1024]{1,0:T(8,128)(2,1)} %collective-permute-done.5.near_half), channel_id=1, source_target_pairs={{0,1},{1,0},{2,3},{3,2},{4,5},{5,4},{6,7},{7,6},{8,9},{9,8},{10,11... | collective-permute-start | bytes 786440 | tf_op jit(solution)/shard_map/ppermute | solution.py:177
  63.3 0.1 pad_add_fusion.core
  63.4 0.0 collective-permute-done.2
  63.4 0.0 collective-permute-done.1
  63.4 0.0 collective-permute-done
  63.4 0.0 all-to-all-done
  63.4 1.5 %reshape.20.tokens = bf16[256,2048]{1,0:T(8,128)(2,1)S(1)} reshape(bf16[128,2,2048]{2,1,0:T(2,128)(2,1)} %all-to-all-done) | data formatting | bytes 2097152 | tf_op jit(solution)/shard_map/reshape | solution.py:175
  64.9 0.2 collective-permute-done.6.far_half
  65.1 0.0 collective-permute-done.4.far
  65.1 0.0 copy-start
  65.1 1.6 %copy-done = bf16[128,8192]{1,0:T(8,128)(2,1)S(1)} copy-done((bf16[128,8192]{1,0:T(8,128)(2,1)S(1)}, bf16[128,8192]{1,0:T(8,128)(2,1)}, u32[]{:S(2)}) %copy-start) | copy-done | bytes 2097176
  66.7 12.4 %shard_map.55 = f32[64,128]{1,0:T(8,128)S(1)} custom-call(s32[64,128]{1,0:T(8,128)S(1)} %get-tuple-element.6.index, s32[2]{0:T(128)S(1)} %pad_add_fusion.core, bf16[4,128,256]{2,1,0:T(8,128)(2,1)S(1)} %pad_maximum_fusion.grads, bf16[256,2048]{1,0:T(8,128)(2,1)S(1)} %reshape.20.tokens, bf16[128,8192]{1,0:T(8,128)(2,1)S(1)} %copy-done, ...), custom_call_target="tpu_custom_call" | custom-call | tf_op jit(solution)/shard_map/pallas_call | solution.py:122
  79.1 0.1 reshape.21
  79.2 23.6 %all_to_all.10 = f32[128,1,64]{2,1,0:T(1,128)S(1)} all-to-all(f32[128,1,64]{2,1,0:T(1,128)S(1)} %bitcast.20), channel_id=1, replica_groups=mesh['param'=128,'ex'=4] {'param'}, dimensions={0} | all-to-all | bytes 65536 | tf_op jit(solution)/shard_map/all_to_all | solution.py:196
  102.8 0.7 reduce_sum.11
  (4 shorter events, 0.1 us)
Async XLA Ops:
  0.8 25.5 %copy-start.1 = (bf16[1,256,128]{2,1,0:T(8,128)(2,1)S(1)}, bf16[1,256,128]{2,1,0:T(8,128)(2,1)}, u32[]{:S(2)}) copy-start(bf16[1,256,128]{2,1,0:T(8,128)(2,1)} %param.6) | copy-start | bytes 196612
  2.9 36.1 %copy-start.2 = (s32[8192]{0:T(1024)S(1)}, s32[8192]{0:T(1024)}, u32[]{:S(2)}) copy-start(s32[8192]{0:T(1024)} %param.9) | copy-start | bytes 98308
  2.9 36.1 %copy-start.3 = (s32[8192]{0:T(1024)S(1)}, s32[8192]{0:T(1024)}, u32[]{:S(2)}) copy-start(s32[8192]{0:T(1024)} %param.8) | copy-start | bytes 98308
  2.9 60.6 %all-to-all-start = ((bf16[128,2,2048]{2,1,0:T(2,128)(2,1)}), bf16[128,2,2048]{2,1,0:T(2,128)(2,1)}, u32[]{:S(2)}, u32[]{:S(2)}) async-start(bf16[128,2,2048]{2,1,0:T(2,128)(2,1)} %bitcast.11), calls=%async_computation | async-start | bytes 2097152 | tf_op jit(solution)/shard_map/all_to_all | solution.py:174
  23.9 32.4 %collective-permute-start.3 = (bf16[128,2048]{1,0:T(8,128)(2,1)S(1)}, bf16[128,2048]{1,0:T(8,128)(2,1)}, u32[]{:S(2)}, u32[]{:S(2)}) collective-permute-start(bf16[128,2048]{1,0:T(8,128)(2,1)S(1)} %constant_dynamic-slice_fusion.1), channel_id=1, source_target_pairs={{0,32},{1,5},{2,34},{3,7},{4,36},{5,1},{6,38},{7,3},{8,40},{9,13},... | collective-permute-start | bytes 1572872 | tf_op jit(solution)/shard_map/ppermute | solution.py:166
  26.5 36.9 %collective-permute-start.2 = (bf16[128,256]{1,0:T(8,128)(2,1)S(1)}, bf16[128,256]{1,0:T(8,128)(2,1)S(1)}, u32[]{:S(2)}, u32[]{:S(2)}) collective-permute-start(bf16[128,256]{1,0:T(8,128)(2,1)S(1)} %bitcast.21), channel_id=1, source_target_pairs={{0,36},{1,37},{2,38},{3,39},{4,32},{5,33},{6,34},{7,35},{8,44},{9,... | collective-permute-start | bytes 196616 | tf_op jit(solution)/shard_map/ppermute | solution.py:166
  29.6 33.8 %collective-permute-start.1 = (bf16[128,256]{1,0:T(8,128)(2,1)S(1)}, bf16[128,256]{1,0:T(8,128)(2,1)S(1)}, u32[]{:S(2)}, u32[]{:S(2)}) collective-permute-start(bf16[128,256]{1,0:T(8,128)(2,1)S(1)} %bitcast.22), channel_id=1, source_target_pairs={{0,32},{1,33},{2,34},{3,35},{4,36},{5,37},{6,38},{7,39},{8,40},{9,... | collective-permute-start | bytes 196616 | tf_op jit(solution)/shard_map/ppermute | solution.py:166
  32.4 30.9 %collective-permute-start = (bf16[128,256]{1,0:T(8,128)(2,1)S(1)}, bf16[128,256]{1,0:T(8,128)(2,1)S(1)}, u32[]{:S(2)}, u32[]{:S(2)}) collective-permute-start(bf16[128,256]{1,0:T(8,128)(2,1)S(1)} %bitcast.23), channel_id=1, source_target_pairs={{0,4},{1,5},{2,6},{3,7},{4,0},{5,1},{6,2},{7,3},{8,12},{9,13},{10,... | collective-permute-start | bytes 196616 | tf_op jit(solution)/shard_map/ppermute | solution.py:166
  35.8 25.5 %collective-permute-start.5 = (bf16[128,1024]{1,0:T(8,128)(2,1)S(1)}, bf16[128,1024]{1,0:T(8,128)(2,1)}, u32[]{:S(2)}, u32[]{:S(2)}) collective-permute-start(bf16[128,1024]{1,0:T(8,128)(2,1)S(1)} %constant_dynamic-slice_fusion), channel_id=1, source_target_pairs={{0,36},{1,37},{2,38},{3,39},{4,32},{5,33},{6,34},{7,35},{8,44},{9,... | collective-permute-start | bytes 786440 | tf_op jit(solution)/shard_map/ppermute | solution.py:166
  56.3 8.8 %collective-permute-start.4 = (bf16[128,2048]{1,0:T(8,128)(2,1)}, bf16[128,2048]{1,0:T(8,128)(2,1)}, u32[]{:S(2)}, u32[]{:S(2)}) collective-permute-start(bf16[128,2048]{1,0:T(8,128)(2,1)} %collective-permute-done.3.near), channel_id=1, source_target_pairs={{0,1},{1,0},{2,3},{3,2},{4,5},{5,4},{6,7},{7,6},{8,9},{9,8},{10,11... | collective-permute-start | bytes 1572872 | tf_op jit(solution)/shard_map/ppermute | solution.py:176
  61.4 3.8 %collective-permute-start.6 = (bf16[128,1024]{1,0:T(8,128)(2,1)}, bf16[128,1024]{1,0:T(8,128)(2,1)}, u32[]{:S(2)}, u32[]{:S(2)}) collective-permute-start(bf16[128,1024]{1,0:T(8,128)(2,1)} %collective-permute-done.5.near_half), channel_id=1, source_target_pairs={{0,1},{1,0},{2,3},{3,2},{4,5},{5,4},{6,7},{7,6},{8,9},{9,8},{10,11... | collective-permute-start | bytes 786440 | tf_op jit(solution)/shard_map/ppermute | solution.py:177
  65.1 1.6 %copy-start = (bf16[128,8192]{1,0:T(8,128)(2,1)S(1)}, bf16[128,8192]{1,0:T(8,128)(2,1)}, u32[]{:S(2)}) copy-start(bf16[128,8192]{1,0:T(8,128)(2,1)} %own.1) | copy-start | bytes 6291460
where the time goes:
time: 104 us; the launch traced here: 103 us
  starting transfers between devices  37.6 us (36%)
  blocking collectives  23.6 us (23%)
  waiting for transfers between devices  19.3 us (19%)
  Pallas kernels  12.4 us (12%)
  local copies, waits for them, and re-layouts  8.15 us (8%)
  other arithmetic  2.16 us (2%)
    all_to_all x1, blocking collectives, shards(): lax.all_to_all(picked.reshape(parts, 1, -1), 'param', 0, 0, tiled=True)  23.6 us
    all_to_all x1, starting transfers between devices, shards(): lax.all_to_all(tokens.reshape(parts, -1, span), 'param', 0, 0, tiled=True)  19.9 us
    ppermute x5, waiting for transfers between devices, send(): return lax.ppermute(value, ('param', 'ex'), pairs)  19.1 us
    ppermute x5, starting transfers between devices, send(): return lax.ppermute(value, ('param', 'ex'), pairs)  13.9 us
    pallas_call x1, Pallas kernels, local_call(): pl.pallas_call(functools.partial(kernel, norm), out_shape=jax.ShapeDtypeS...  12.4 us
  transfers between devices with their start and end apart: 8, of which 3 were waited for; matrix products, arithmetic and copies ran while one was open for 5% of the time, Pallas kernels for 0%

commit v1 on v0

--- a/solution.py
+++ b/solution.py
@@ -31,30 +31,44 @@
     return parts
 
 
-def kernel(norm, index, core, grads, tokens, own, near, far, near_half, far_half, table, rows_sign, out, *scratch):
-    block, even, odd, own_v, near_v, far_v, near_half_v, far_half_v, here, later, arrived, listed = scratch
+def kernel(norm, index, core, grads, tokens, own, z_mine, z_other, x_mine, x_other, table, rows_sign, out, *scratch):
+    block, even, odd, signs, picks, here, later, arrived, listed = scratch
     rows = grads.shape[1]
     me = core[0]
     span = tokens.shape[1]
     group = here.shape[0]
     groups = index.shape[0] // group
-    sources = (own.at[:, pl.ds(pl.multiple_of(core[1] * span, span), span)], near, far, near_half, far_half)
-    signs = (own_v, near_v, far_v, near_half_v, far_half_v)
-    copies = [pltpu.make_async_copy(a, b, arrived.at[i]) for i, (a, b) in enumerate(zip(sources, signs))]
+
+    def load(source, place):
+        return pltpu.make_async_copy(source, signs.at[place], arrived.at[place])
+
+    columns = pl.ds(pl.multiple_of(core[1] * span, span), span)
+    copies = (load(own.at[:, columns], 0), load(z_mine, 1), load(x_mine, 2), load(x_other, 3))
 
     def fetch(i, part, places):
         start = pl.multiple_of(i * group, group)
         return pltpu.make_async_copy(index.at[pl.ds(start, group)], places, listed.at[part])
 
-    for copy in copies:
-        copy.start()
+    for i in (0, 2, 3):
+        copies[i].start()
+
+    @pl.when(me == 0)
+    def _():
+        copies[1].start()
+
+    @pl.when(me != 0)
+    def _():
+        load(z_other, 1).start()
+
+    picking = pltpu.make_async_copy(table, picks, listed.at[2])
+    picking.start()
     fetch(0, 0, here).start()
     fetch(1, 1, later).start()
 
-    def chunk(signs, start, slot, half):
+    def chunk(place, slot, half):
         cols = pl.ds(pl.multiple_of(half * STEP, STEP), STEP)
         g = jnp.dot(grads[slot], tokens[:, cols], preferred_element_type=jnp.float32)
-        f = g * signs[:, pl.ds(pl.multiple_of(start, STEP), STEP)].astype(jnp.float32)
+        f = g * signs[place, :, cols].astype(jnp.float32)
         r = jnp.dot(rows_sign[...], jnp.concatenate(split(f), 0), preferred_element_type=jnp.float32)
         for t in range(rows // 8):
             parts = butterfly([r[8 * t : 8 * t + 8, LANES * u : LANES * u + LANES] for u in range(8)])
@@ -62,15 +76,12 @@
                 base = ((slot * 2 + half) * 8 + u) * rows + 8 * t
                 block[pl.ds(pl.multiple_of(base, 8), 8), :] = parts[u]
 
-    for i, slot in enumerate((0, 2 - me, 1 + me)):
+    for i, slot in enumerate((0, 1, 2 + me, 3 - me)):
         copies[i].wait()
 
         @pl.loop(0, 2)
         def _(half):
-            chunk(signs[i], half * STEP, slot, half)
-    for i, half in ((3, me), (4, 1 - me)):
-        copies[i].wait()
-        chunk(signs[i], 0, 3, half)
+            chunk(i, slot, half)
 
     @pl.loop(0, rows // 8)
     def _(t):
@@ -87,13 +98,14 @@
             picked[pl.ds(s, 1), :] = block[pl.ds(places[row, s], 1), :]
 
     def select(b, picked):
-        m = table[b]
+        m = picks[b]
         z = jnp.dot(
             jnp.concatenate(split(picked[...]), 1), jnp.concatenate([m, m], 0), preferred_element_type=jnp.float32
         )
         out[pl.ds(b, 1), :] = jnp.sum(jnp.where(eye, z, 0.0), axis=0, keepdims=True) * norm
 
     buffers = (even, odd)
+    picking.wait()
 
     @pl.loop(0, groups // 2)
     def _(i):
@@ -112,29 +124,28 @@
             select(g * group + group - 1, buffers[1 - group % 2])
 
 
-def local_call(norm, index, core, grads, tokens, own, near, far, near_half, far_half, table):
+def local_call(norm, index, core, grads, tokens, signs, table):
     rows = grads.shape[1]
     h = hadamard_table(rows)
-    smem, vmem, held = (pl.BlockSpec(memory_space=m) for m in (pltpu.SMEM, pltpu.VMEM, pl.ANY))
+    smem, vmem, held = (pl.BlockSpec(memory_space=m) for m in (pltpu.SMEM, pltpu.VMEM, pltpu.HBM))
     places = pltpu.SMEM((8, LANES), jnp.int32)
-    signs = (own, near, far, near_half, far_half)
-    widths = (near.shape[1],) * 3 + (near_half.shape[1],) * 2
     return pl.pallas_call(
         functools.partial(kernel, norm),
         out_shape=jax.ShapeDtypeStruct(index.shape, jnp.float32),
-        in_specs=[vmem, smem, vmem, vmem] + [held] * 5 + [vmem, vmem],
+        in_specs=[vmem, smem, vmem, vmem] + [held] * 6 + [vmem],
         out_specs=vmem,
         scratch_shapes=[
             pltpu.VMEM((grads.shape[0] * rows * tokens.shape[1] // LANES, LANES), jnp.float32),
             pltpu.VMEM((LANES, LANES), jnp.float32),
             pltpu.VMEM((LANES, LANES), jnp.float32),
-            *(pltpu.VMEM((rows, w), own.dtype) for w in widths),
+            pltpu.VMEM((4, rows, tokens.shape[1]), signs[0].dtype),
+            pltpu.VMEM(table.shape, table.dtype),
             places,
             places,
-            pltpu.SemaphoreType.DMA((len(signs),)),
-            pltpu.SemaphoreType.DMA((2,)),
+            pltpu.SemaphoreType.DMA((4,)),
+            pltpu.SemaphoreType.DMA((3,)),
         ],
-        compiler_params=pltpu.CompilerParams(vmem_limit_bytes=40 << 20),
+        compiler_params=pltpu.CompilerParams(vmem_limit_bytes=50 << 20),
     )(index, core, grads, tokens, *signs, table, jnp.concatenate([h, h], 1))
 
 
@@ -158,27 +169,28 @@
     def columns(start_place, start, size):
         return lax.dynamic_slice_in_dim(sign_flips, start_place * span + start, size, 1)
 
-    def send(value, slot_of_core):
-        pairs = [
-            (p * examples + e, (p ^ shift[slot_of_core[e % cores]]) * examples + e)
-            for p in range(ys * xs * zs) for e in range(examples)
-        ]
+    def send(value, slot, cross=False):
+        pairs = []
+        for p in range(ys * xs * zs):
+            for e in range(examples):
+                to = e ^ cores if cross and e % cores else e
+                pairs.append((p * examples + e, (p ^ shift[slot]) * examples + to))
         return lax.ppermute(value, ("param", "ex"), pairs)
 
     swap = [(e, e ^ 1) for e in range(examples)]
 
-    near = send(columns(place ^ (2 - core), 0, span), (2, 1))
-    near_half = send(columns(place ^ 3, core * (span // 2), span // 2), (3, 3))
+    z_mine = send(columns(place ^ (1 + 2 * core), 0, span), 1)
+    x_mine = send(jnp.where(core == 0, columns(place ^ 2, 0, span), z_mine), 2, True)
     tokens = inputs[0].reshape(-1, xs, 2, span).transpose(1, 2, 0, 3)
     tokens = jnp.broadcast_to(tokens[None, :, None], (ys, xs, zs // 2, 2) + tokens.shape[2:])
     tokens = lax.all_to_all(tokens.reshape(parts, -1, span), "param", 0, 0, tiled=True)
     tokens = tokens.reshape(-1, span)
-    far = lax.ppermute(near, "ex", swap)
-    far_half = lax.ppermute(near_half, "ex", swap)
+    z_other = lax.ppermute(z_mine, "ex", swap)
+    x_other = lax.ppermute(x_mine, "ex", swap)
     grad = cotangents[0].T
     grads = [grad]
     for s in (1, 2, 3):
-        grads.append(send(grad, (s, s)))
+        grads.append(send(grad, s))
     grads = jnp.stack(grads)
 
     owner, row = sample_rows // rows, sample_rows % rows
@@ -191,7 +203,7 @@
     table = (1 - 2 * (odd & 1)).astype(jnp.bfloat16)
 
     picked = local_call(
-        norm, index, jnp.stack([core, place]), grads, tokens, sign_flips, near, far, near_half, far_half, table
+        norm, index, jnp.stack([core, place]), grads, tokens, (sign_flips, z_mine, z_other, x_mine, x_other), table
     )
     return lax.all_to_all(picked.reshape(parts, 1, -1), "param", 0, 0, tiled=True).sum(0)
 

time: 104 us -> 118 us (1.13)
  the two profiles are of different devices: /device:TPU:1 before, /device:TPU:4 now
where the time goes in v1:
time: 118 us; the launch traced here: 117 us
  starting transfers between devices  39 us (33%)
  waiting for transfers between devices  31.4 us (27%)
  blocking collectives  25 us (21%)
  Pallas kernels  13.2 us (11%)
  local copies, waits for them, and re-layouts  4.7 us (4%)
  other arithmetic  3.62 us (3%)
    ppermute x5, waiting for transfers between devices, send(): return lax.ppermute(value, ('param', 'ex'), pairs)  31.4 us
    all_to_all x1, blocking collectives, shards(): lax.all_to_all(picked.reshape(parts, 1, -1), 'param', 0, 0, tiled=True)  25 us
    all_to_all x1, starting transfers between devices, shards(): lax.all_to_all(tokens.reshape(parts, -1, span), 'param', 0, 0, tiled=True)  19.1 us
    ppermute x5, starting transfers between devices, send(): return lax.ppermute(value, ('param', 'ex'), pairs)  15.6 us
    pallas_call x1, Pallas kernels, local_call(): pl.pallas_call(functools.partial(kernel, norm), out_shape=jax.ShapeDtypeS...  13.2 us
    convert_element_type x1, other arithmetic, shards(): table = (1 - 2 * (odd & 1)).astype(jnp.bfloat16)  2.59 us
    ppermute x1, starting transfers between devices, shards(): x_other = lax.ppermute(x_mine, 'ex', swap)  2.41 us
  transfers between devices with their start and end apart: 8, of which 1 were waited for; matrix products, arithmetic and copies ran while one was open for 4% of the time, Pallas kernels for 0%

profile of v1, /device:TPU:4, one launch (start us, length us, event | category | flops | bytes accessed | tf_op | source)
XLA Modules:
  0.0 117.2 jit_solution(3902652932113223905)
XLA Ops:
  0.0 0.0 copy-start
  0.0 0.9 reshape_squeeze.3
  1.0 2.0 %broadcast_in_dim.2 = bf16[8,2,4,2,2,2048]{5,4,3,2,1,0:T(2,128)(2,1)} broadcast(bf16[2,2,2,2048]{3,2,1,0:T(2,128)(2,1)S(1)} %copy.11), dimensions={1,3,4,5} | broadcast | bytes 1081344 | tf_op jit(solution)/shard_map/broadcast_in_dim | solution.py:185
  3.0 0.0 copy-start.1
  3.0 0.0 copy-start.2
  3.0 0.0 copy-start.3
  3.0 19.1 %all-to-all-start = ((bf16[128,2,2048]{2,1,0:T(2,128)(2,1)}), bf16[128,2,2048]{2,1,0:T(2,128)(2,1)}, u32[]{:S(2)}, u32[]{:S(2)}) async-start(bf16[128,2,2048]{2,1,0:T(2,128)(2,1)} %bitcast.20), calls=%async_computation | async-start | bytes 2097152 | tf_op jit(solution)/shard_map/all_to_all | solution.py:186
  22.1 0.0 copy-done
  22.2 3.0 %collective-permute-start.3 = (bf16[128,2048]{1,0:T(8,128)(2,1)S(1)}, bf16[128,2048]{1,0:T(8,128)(2,1)S(1)}, u32[]{:S(2)}, u32[]{:S(2)}) collective-permute-start(bf16[128,2048]{1,0:T(8,128)(2,1)S(1)} %constant_dynamic-slice_fusion), channel_id=1, source_target_pairs={{0,4},{1,5},{2,6},{3,7},{4,0},{5,1},{6,2},{7,3},{8,12},{9,13},{10,... | collective-permute-start | bytes 1572872 | tf_op jit(solution)/shard_map/ppermute | solution.py:178
  25.2 31.4 %collective-permute-done.3.z_mine = bf16[128,2048]{1,0:T(8,128)(2,1)S(1)} collective-permute-done((bf16[128,2048]{1,0:T(8,128)(2,1)S(1)}, bf16[128,2048]{1,0:T(8,128)(2,1)S(1)}, u32[]{:S(2)}, u32[]{:S(2)}) %collective-permute-start.3) | collective-permute-done | bytes 524320 | tf_op jit(solution)/shard_map/ppermute | solution.py:178
  56.6 0.1 dynamic-slice_select_fusion
  56.7 3.4 %collective-permute-start.5 = (bf16[128,2048]{1,0:T(8,128)(2,1)S(1)}, bf16[128,2048]{1,0:T(8,128)(2,1)S(1)}, u32[]{:S(2)}, u32[]{:S(2)}) collective-permute-start(bf16[128,2048]{1,0:T(8,128)(2,1)S(1)} %dynamic-slice_select_fusion), channel_id=1, source_target_pairs={{0,32},{1,35},{2,34},{3,33},{4,36},{5,39},{6,38},{7,37},{8,40},{9,... | collective-permute-start | bytes 1572872 | tf_op jit(solution)/shard_map/ppermute | solution.py:178
  60.1 0.0 copy-done.1
  60.1 0.1 copy.10
  60.2 3.2 %collective-permute-start.2 = (bf16[128,256]{1,0:T(8,128)(2,1)S(1)}, bf16[128,256]{1,0:T(8,128)(2,1)S(1)}, u32[]{:S(2)}, u32[]{:S(2)}) collective-permute-start(bf16[128,256]{1,0:T(8,128)(2,1)S(1)} %bitcast.22), channel_id=1, source_target_pairs={{0,36},{1,37},{2,38},{3,39},{4,32},{5,33},{6,34},{7,35},{8,44},{9,... | collective-permute-start | bytes 196616 | tf_op jit(solution)/shard_map/ppermute | solution.py:178
  63.5 3.0 %collective-permute-start.1 = (bf16[128,256]{1,0:T(8,128)(2,1)S(1)}, bf16[128,256]{1,0:T(8,128)(2,1)S(1)}, u32[]{:S(2)}, u32[]{:S(2)}) collective-permute-start(bf16[128,256]{1,0:T(8,128)(2,1)S(1)} %bitcast.23), channel_id=1, source_target_pairs={{0,32},{1,33},{2,34},{3,35},{4,36},{5,37},{6,38},{7,39},{8,40},{9,... | collective-permute-start | bytes 196616 | tf_op jit(solution)/shard_map/ppermute | solution.py:178
  66.4 3.0 %collective-permute-start = (bf16[128,256]{1,0:T(8,128)(2,1)S(1)}, bf16[128,256]{1,0:T(8,128)(2,1)S(1)}, u32[]{:S(2)}, u32[]{:S(2)}) collective-permute-start(bf16[128,256]{1,0:T(8,128)(2,1)S(1)} %bitcast.24), channel_id=1, source_target_pairs={{0,4},{1,5},{2,6},{3,7},{4,0},{5,1},{6,2},{7,3},{8,12},{9,13},{10,... | collective-permute-start | bytes 196616 | tf_op jit(solution)/shard_map/ppermute | solution.py:178
  69.5 0.0 copy-done.2
  69.5 0.0 copy-done.3
  69.5 0.1 fusion.10
  69.6 1.9 %collective-permute-start.4 = (bf16[128,2048]{1,0:T(8,128)(2,1)S(1)}, bf16[128,2048]{1,0:T(8,128)(2,1)S(1)}, u32[]{:S(2)}, u32[]{:S(2)}) collective-permute-start(bf16[128,2048]{1,0:T(8,128)(2,1)S(1)} %collective-permute-done.3.z_mine), channel_id=1, source_target_pairs={{0,1},{1,0},{2,3},{3,2},{4,5},{5,4},{6,7},{7,6},{8,9},{9,8},{10,11... | collective-permute-start | bytes 1572872 | tf_op jit(solution)/shard_map/ppermute | solution.py:188
  71.6 0.0 collective-permute-done.5.x_mine
  71.6 2.4 %collective-permute-start.6 = (bf16[128,2048]{1,0:T(8,128)(2,1)S(1)}, bf16[128,2048]{1,0:T(8,128)(2,1)S(1)}, u32[]{:S(2)}, u32[]{:S(2)}) collective-permute-start(bf16[128,2048]{1,0:T(8,128)(2,1)S(1)} %collective-permute-done.5.x_mine), channel_id=1, source_target_pairs={{0,1},{1,0},{2,3},{3,2},{4,5},{5,4},{6,7},{7,6},{8,9},{9,8},{10,11... | collective-permute-start | bytes 1572872 | tf_op jit(solution)/shard_map/ppermute | solution.py:189
  74.0 2.6 %subtract_convert_fusion.table = bf16[64,128,128]{2,1,0:T(8,128)(2,1)} fusion(s32[64,128]{1,0:T(8,128)S(1)} %get-tuple-element.7, s32[64,128]{1,0:T(8,128)S(1)} %get-tuple-element.5), kind=kLoop, calls=%fused_computation | loop fusion | flops 8388608 | bytes 2162688 | tf_op jit(solution)/shard_map/convert_element_type | solution.py:203
  76.6 0.1 pad_add_fusion.core
  76.6 0.0 collective-permute-done.2
  76.6 0.0 collective-permute-done.1
  76.7 0.0 collective-permute-done
  76.7 0.0 all-to-all-done
  76.7 1.5 %reshape.20.tokens = bf16[256,2048]{1,0:T(8,128)(2,1)S(1)} reshape(bf16[128,2,2048]{2,1,0:T(2,128)(2,1)} %all-to-all-done) | data formatting | bytes 2097152 | tf_op jit(solution)/shard_map/reshape | solution.py:187
  78.2 0.0 collective-permute-done.4.z_other
  78.2 0.0 collective-permute-done.6.x_other
  78.2 13.2 %shard_map.55 = f32[64,128]{1,0:T(8,128)S(1)} custom-call(s32[64,128]{1,0:T(8,128)S(1)} %get-tuple-element.6.index, s32[2]{0:T(128)S(1)} %pad_add_fusion.core, bf16[4,128,256]{2,1,0:T(8,128)(2,1)S(1)} %pad_maximum_fusion.grads, bf16[256,2048]{1,0:T(8,128)(2,1)S(1)} %reshape.20.tokens, bf16[128,8192]{1,0:T(8,128)(2,1)} %own.1, ...), custom_call_target="tpu_custom_call" | custom-call | tf_op jit(solution)/shard_map/pallas_call | solution.py:132
  91.5 0.1 reshape.21
  91.5 25.0 %all_to_all.10 = f32[128,1,64]{2,1,0:T(1,128)S(1)} all-to-all(f32[128,1,64]{2,1,0:T(1,128)S(1)} %bitcast.21), channel_id=1, replica_groups=mesh['param'=128,'ex'=4] {'param'}, dimensions={0} | all-to-all | bytes 65536 | tf_op jit(solution)/shard_map/all_to_all | solution.py:208
  116.6 0.7 reduce_sum.11
  (5 shorter events, 0.1 us)
Async XLA Ops:
  0.0 22.1 %copy-start = (bf16[128,8192]{1,0:T(8,128)(2,1)S(1)}, bf16[128,8192]{1,0:T(8,128)(2,1)}, u32[]{:S(2)}) copy-start(bf16[128,8192]{1,0:T(8,128)(2,1)} %own.1) | copy-start | bytes 6291460
  3.0 57.1 %copy-start.1 = (bf16[1,256,128]{2,1,0:T(8,128)(2,1)S(1)}, bf16[1,256,128]{2,1,0:T(8,128)(2,1)}, u32[]{:S(2)}) copy-start(bf16[1,256,128]{2,1,0:T(8,128)(2,1)} %param.6) | copy-start | bytes 196612
  3.0 66.5 %copy-start.2 = (s32[8192]{0:T(1024)S(1)}, s32[8192]{0:T(1024)}, u32[]{:S(2)}) copy-start(s32[8192]{0:T(1024)} %param.9) | copy-start | bytes 98308
  3.0 66.5 %copy-start.3 = (s32[8192]{0:T(1024)S(1)}, s32[8192]{0:T(1024)}, u32[]{:S(2)}) copy-start(s32[8192]{0:T(1024)} %param.8) | copy-start | bytes 98308
  3.0 73.7 %all-to-all-start = ((bf16[128,2,2048]{2,1,0:T(2,128)(2,1)}), bf16[128,2,2048]{2,1,0:T(2,128)(2,1)}, u32[]{:S(2)}, u32[]{:S(2)}) async-start(bf16[128,2,2048]{2,1,0:T(2,128)(2,1)} %bitcast.20), calls=%async_computation | async-start | bytes 2097152 | tf_op jit(solution)/shard_map/all_to_all | solution.py:186
  22.2 34.4 %collective-permute-start.3 = (bf16[128,2048]{1,0:T(8,128)(2,1)S(1)}, bf16[128,2048]{1,0:T(8,128)(2,1)S(1)}, u32[]{:S(2)}, u32[]{:S(2)}) collective-permute-start(bf16[128,2048]{1,0:T(8,128)(2,1)S(1)} %constant_dynamic-slice_fusion), channel_id=1, source_target_pairs={{0,4},{1,5},{2,6},{3,7},{4,0},{5,1},{6,2},{7,3},{8,12},{9,13},{10,... | collective-permute-start | bytes 1572872 | tf_op jit(solution)/shard_map/ppermute | solution.py:178
  56.7 14.8 %collective-permute-start.5 = (bf16[128,2048]{1,0:T(8,128)(2,1)S(1)}, bf16[128,2048]{1,0:T(8,128)(2,1)S(1)}, u32[]{:S(2)}, u32[]{:S(2)}) collective-permute-start(bf16[128,2048]{1,0:T(8,128)(2,1)S(1)} %dynamic-slice_select_fusion), channel_id=1, source_target_pairs={{0,32},{1,35},{2,34},{3,33},{4,36},{5,39},{6,38},{7,37},{8,40},{9,... | collective-permute-start | bytes 1572872 | tf_op jit(solution)/shard_map/ppermute | solution.py:178
  60.2 16.4 %collective-permute-start.2 = (bf16[128,256]{1,0:T(8,128)(2,1)S(1)}, bf16[128,256]{1,0:T(8,128)(2,1)S(1)}, u32[]{:S(2)}, u32[]{:S(2)}) collective-permute-start(bf16[128,256]{1,0:T(8,128)(2,1)S(1)} %bitcast.22), channel_id=1, source_target_pairs={{0,36},{1,37},{2,38},{3,39},{4,32},{5,33},{6,34},{7,35},{8,44},{9,... | collective-permute-start | bytes 196616 | tf_op jit(solution)/shard_map/ppermute | solution.py:178
  63.5 13.2 %collective-permute-start.1 = (bf16[128,256]{1,0:T(8,128)(2,1)S(1)}, bf16[128,256]{1,0:T(8,128)(2,1)S(1)}, u32[]{:S(2)}, u32[]{:S(2)}) collective-permute-start(bf16[128,256]{1,0:T(8,128)(2,1)S(1)} %bitcast.23), channel_id=1, source_target_pairs={{0,32},{1,33},{2,34},{3,35},{4,36},{5,37},{6,38},{7,39},{8,40},{9,... | collective-permute-start | bytes 196616 | tf_op jit(solution)/shard_map/ppermute | solution.py:178
  66.4 10.2 %collective-permute-start = (bf16[128,256]{1,0:T(8,128)(2,1)S(1)}, bf16[128,256]{1,0:T(8,128)(2,1)S(1)}, u32[]{:S(2)}, u32[]{:S(2)}) collective-permute-start(bf16[128,256]{1,0:T(8,128)(2,1)S(1)} %bitcast.24), channel_id=1, source_target_pairs={{0,4},{1,5},{2,6},{3,7},{4,0},{5,1},{6,2},{7,3},{8,12},{9,13},{10,... | collective-permute-start | bytes 196616 | tf_op jit(solution)/shard_map/ppermute | solution.py:178
  69.6 8.6 %collective-permute-start.4 = (bf16[128,2048]{1,0:T(8,128)(2,1)S(1)}, bf16[128,2048]{1,0:T(8,128)(2,1)S(1)}, u32[]{:S(2)}, u32[]{:S(2)}) collective-permute-start(bf16[128,2048]{1,0:T(8,128)(2,1)S(1)} %collective-permute-done.3.z_mine), channel_id=1, source_target_pairs={{0,1},{1,0},{2,3},{3,2},{4,5},{5,4},{6,7},{7,6},{8,9},{9,8},{10,11... | collective-permute-start | bytes 1572872 | tf_op jit(solution)/shard_map/ppermute | solution.py:188
  71.6 6.6 %collective-permute-start.6 = (bf16[128,2048]{1,0:T(8,128)(2,1)S(1)}, bf16[128,2048]{1,0:T(8,128)(2,1)S(1)}, u32[]{:S(2)}, u32[]{:S(2)}) collective-permute-start(bf16[128,2048]{1,0:T(8,128)(2,1)S(1)} %collective-permute-done.5.x_mine), channel_id=1, source_target_pairs={{0,1},{1,0},{2,3},{3,2},{4,5},{5,4},{6,7},{7,6},{8,9},{9,8},{10,11... | collective-permute-start | bytes 1572872 | tf_op jit(solution)/shard_map/ppermute | solution.py:189

commit v2 on v1

--- a/solution.py
+++ b/solution.py
@@ -7,6 +7,8 @@
 
 LANES = 128
 STEP = 8 * LANES
+TILES = 2 * STEP // LANES
+ROOM = 50 << 20
 
 
 def hadamard_table(order):
@@ -31,44 +33,108 @@
     return parts
 
 
-def kernel(norm, index, core, grads, tokens, own, z_mine, z_other, x_mine, x_other, table, rows_sign, out, *scratch):
-    block, even, odd, signs, picks, here, later, arrived, listed = scratch
-    rows = grads.shape[1]
+def tiles(signs, start, places, arrived):
+    return [
+        pltpu.make_async_copy(
+            signs.at[:, pl.ds(pl.multiple_of(start + i * LANES, LANES), LANES)], places.at[i], arrived.at[i]
+        )
+        for i in range(TILES)
+    ]
+
+
+def first_kernel(start, tokens, signs, grads, parcel, spread, staged, arrived, sent):
+    loads = tiles(signs, start[0], parcel, arrived)
+    loads.append(pltpu.make_async_copy(grads, parcel.at[pl.ds(TILES, 2)], arrived.at[TILES]))
+    for load in loads:
+        load.start()
+    xs, repeats, zs, _, span = staged.shape
+    for x in range(xs):
+        for z in range(zs):
+            part = tokens[:, (x * zs + z) * span : (x * zs + z + 1) * span]
+            for i in range(repeats):
+                staged[x, i, z] = part
+    stores = [pltpu.make_async_copy(staged, spread.at[y], sent.at[y]) for y in range(spread.shape[0])]
+    for store in stores:
+        store.start()
+    for copy in loads + stores:
+        copy.wait()
+
+
+def second_kernel(core, signs, received, grads, parcel, arrived):
+    own = tiles(signs, core[1], parcel, arrived)
+    relayed = [pltpu.make_async_copy(received.at[i], parcel.at[i], arrived.at[i]) for i in range(TILES)]
+
+    @pl.when(core[0] == 0)
+    def _():
+        for copy in own:
+            copy.start()
+
+    @pl.when(core[0] != 0)
+    def _():
+        for copy in relayed:
+            copy.start()
+
+    more = [
+        pltpu.make_async_copy(grads, parcel.at[pl.ds(TILES, 2)], arrived.at[TILES]),
+        pltpu.make_async_copy(received.at[pl.ds(TILES, 2)], parcel.at[pl.ds(TILES + 2, 2)], arrived.at[TILES + 1]),
+    ]
+    for copy in more:
+        copy.start()
+    for copy in relayed + more:
+        copy.wait()
+
+
+def kernel(norm, index, core, tokens, own, own_grad, z_mine, z_other, x_mine, x_other, table, rows_sign, out, *scratch):
+    block, even, odd, signs, flat, grads, picks, here, later, own_arrived, arrived, listed = scratch
+    rows = own.shape[0]
     me = core[0]
-    span = tokens.shape[1]
     group = here.shape[0]
     groups = index.shape[0] // group
+    own_tiles = tiles(own, core[1], signs.at[0], own_arrived)
 
     def load(source, place):
-        return pltpu.make_async_copy(source, signs.at[place], arrived.at[place])
-
-    columns = pl.ds(pl.multiple_of(core[1] * span, span), span)
-    copies = (load(own.at[:, columns], 0), load(z_mine, 1), load(x_mine, 2), load(x_other, 3))
+        return pltpu.make_async_copy(source.at[pl.ds(0, TILES)], signs.at[place], arrived.at[place])
+
+    def load_grad(source, start, place):
+        return pltpu.make_async_copy(source.at[pl.ds(start, 2)], flat.at[place], arrived.at[4 + place])
+
+    grad_loads = (
+        load_grad(own_grad, 0, 0),
+        load_grad(z_mine, TILES, 1),
+        load_grad(x_mine, TILES, 2),
+        load_grad(x_mine, TILES + 2, 3),
+    )
+    copies = (None, load(z_mine, 1), load(x_mine, 2), load(x_other, 3))
+    for copy in grad_loads + tuple(own_tiles) + copies[2:]:
+        copy.start()
+
+    @pl.when(me == 0)
+    def _():
+        copies[1].start()
+
+    @pl.when(me != 0)
+    def _():
+        load(z_other, 1).start()
 
     def fetch(i, part, places):
         start = pl.multiple_of(i * group, group)
         return pltpu.make_async_copy(index.at[pl.ds(start, group)], places, listed.at[part])
-
-    for i in (0, 2, 3):
-        copies[i].start()
-
-    @pl.when(me == 0)
-    def _():
-        copies[1].start()
-
-    @pl.when(me != 0)
-    def _():
-        load(z_other, 1).start()
 
     picking = pltpu.make_async_copy(table, picks, listed.at[2])
     picking.start()
     fetch(0, 0, here).start()
     fetch(1, 1, later).start()
 
+    for place, copy in enumerate(grad_loads):
+        copy.wait()
+        grads[place] = flat[place].reshape(-1, rows).T
+
     def chunk(place, slot, half):
         cols = pl.ds(pl.multiple_of(half * STEP, STEP), STEP)
         g = jnp.dot(grads[slot], tokens[:, cols], preferred_element_type=jnp.float32)
-        f = g * signs[place, :, cols].astype(jnp.float32)
+        f = jnp.concatenate(
+            [g[:, LANES * u : LANES * u + LANES] * signs[place, half * 8 + u].astype(jnp.float32) for u in range(8)], 1
+        )
         r = jnp.dot(rows_sign[...], jnp.concatenate(split(f), 0), preferred_element_type=jnp.float32)
         for t in range(rows // 8):
             parts = butterfly([r[8 * t : 8 * t + 8, LANES * u : LANES * u + LANES] for u in range(8)])
@@ -77,7 +143,8 @@
                 block[pl.ds(pl.multiple_of(base, 8), 8), :] = parts[u]
 
     for i, slot in enumerate((0, 1, 2 + me, 3 - me)):
-        copies[i].wait()
+        for copy in [copies[i]] if i else own_tiles:
+            copy.wait()
 
         @pl.loop(0, 2)
         def _(half):
@@ -124,29 +191,43 @@
             select(g * group + group - 1, buffers[1 - group % 2])
 
 
-def local_call(norm, index, core, grads, tokens, signs, table):
-    rows = grads.shape[1]
+def copies_call(body, results, where, operands, memory, scratch):
+    return pl.pallas_call(
+        body,
+        out_shape=results,
+        in_specs=[pl.BlockSpec(memory_space=m) for m in memory],
+        out_specs=jax.tree.map(lambda m: pl.BlockSpec(memory_space=m), where),
+        scratch_shapes=scratch,
+        compiler_params=pltpu.CompilerParams(vmem_limit_bytes=54 << 20),
+    )(*operands)
+
+
+def local_call(norm, index, core, tokens, own, own_grad, parcels, table):
+    rows = own.shape[0]
     h = hadamard_table(rows)
     smem, vmem, held = (pl.BlockSpec(memory_space=m) for m in (pltpu.SMEM, pltpu.VMEM, pltpu.HBM))
     places = pltpu.SMEM((8, LANES), jnp.int32)
     return pl.pallas_call(
         functools.partial(kernel, norm),
         out_shape=jax.ShapeDtypeStruct(index.shape, jnp.float32),
-        in_specs=[vmem, smem, vmem, vmem] + [held] * 6 + [vmem],
+        in_specs=[vmem, smem, vmem] + [held] * 7 + [vmem],
         out_specs=vmem,
         scratch_shapes=[
-            pltpu.VMEM((grads.shape[0] * rows * tokens.shape[1] // LANES, LANES), jnp.float32),
+            pltpu.VMEM((4 * rows * tokens.shape[1] // LANES, LANES), jnp.float32),
             pltpu.VMEM((LANES, LANES), jnp.float32),
             pltpu.VMEM((LANES, LANES), jnp.float32),
-            pltpu.VMEM((4, rows, tokens.shape[1]), signs[0].dtype),
+            pltpu.VMEM((4, TILES, rows, LANES), own.dtype),
+            pltpu.VMEM((4,) + own_grad.shape, own_grad.dtype),
+            pltpu.VMEM((4, rows, tokens.shape[0]), own_grad.dtype),
             pltpu.VMEM(table.shape, table.dtype),
             places,
             places,
-            pltpu.SemaphoreType.DMA((4,)),
+            pltpu.SemaphoreType.DMA((TILES,)),
+            pltpu.SemaphoreType.DMA((8,)),
             pltpu.SemaphoreType.DMA((3,)),
         ],
-        compiler_params=pltpu.CompilerParams(vmem_limit_bytes=50 << 20),
-    )(index, core, grads, tokens, *signs, table, jnp.concatenate([h, h], 1))
+        compiler_params=pltpu.CompilerParams(vmem_limit_bytes=ROOM),
+    )(index, core, tokens, own, own_grad, *parcels, table, jnp.concatenate([h, h], 1))
 
 
 def odd_bits(v):
@@ -166,32 +247,44 @@
     place = (own >> 3 & 1) * 2 + (own & 1)
     span = width // 4
 
-    def columns(start_place, start, size):
-        return lax.dynamic_slice_in_dim(sign_flips, start_place * span + start, size, 1)
-
-    def send(value, slot, cross=False):
-        pairs = []
-        for p in range(ys * xs * zs):
-            for e in range(examples):
-                to = e ^ cores if cross and e % cores else e
-                pairs.append((p * examples + e, (p ^ shift[slot]) * examples + to))
+    def send(value, slot):
+        pairs = [
+            (p * examples + e, (p ^ shift[slot]) * examples + e)
+            for p in range(ys * xs * zs)
+            for e in range(examples)
+        ]
         return lax.ppermute(value, ("param", "ex"), pairs)
 
     swap = [(e, e ^ 1) for e in range(examples)]
 
-    z_mine = send(columns(place ^ (1 + 2 * core), 0, span), 1)
-    x_mine = send(jnp.where(core == 0, columns(place ^ 2, 0, span), z_mine), 2, True)
-    tokens = inputs[0].reshape(-1, xs, 2, span).transpose(1, 2, 0, 3)
-    tokens = jnp.broadcast_to(tokens[None, :, None], (ys, xs, zs // 2, 2) + tokens.shape[2:])
-    tokens = lax.all_to_all(tokens.reshape(parts, -1, span), "param", 0, 0, tiled=True)
+    grad = cotangents[0].reshape(2, -1, rows)
+    tile = jax.ShapeDtypeStruct((TILES + 2, rows, LANES), sign_flips.dtype)
+    parcel, spread = copies_call(
+        first_kernel,
+        (tile, jax.ShapeDtypeStruct((ys, xs, zs // 2, 2, inputs.shape[1], span), inputs.dtype)),
+        (pltpu.VMEM, pltpu.HBM),
+        (((place ^ (1 + 2 * core)) * span)[None], inputs[0], sign_flips, grad),
+        (pltpu.SMEM, pltpu.VMEM, pltpu.HBM, pltpu.HBM),
+        [
+            pltpu.VMEM((xs, zs // 2, 2, inputs.shape[1], span), inputs.dtype),
+            pltpu.SemaphoreType.DMA((TILES + 1,)),
+            pltpu.SemaphoreType.DMA((ys,)),
+        ],
+    )
+    z_mine = send(parcel, 1)
+    tokens = lax.all_to_all(spread.reshape(parts, -1, span), "param", 0, 0, tiled=True)
     tokens = tokens.reshape(-1, span)
+    parcel = copies_call(
+        second_kernel,
+        jax.ShapeDtypeStruct((TILES + 4, rows, LANES), sign_flips.dtype),
+        pltpu.VMEM,
+        (jnp.stack([core, (place ^ 2) * span]), sign_flips, z_mine, grad),
+        (pltpu.SMEM, pltpu.HBM, pltpu.HBM, pltpu.HBM),
+        [pltpu.SemaphoreType.DMA((TILES + 2,))],
+    )
+    x_mine = send(parcel, 2)
     z_other = lax.ppermute(z_mine, "ex", swap)
     x_other = lax.ppermute(x_mine, "ex", swap)
-    grad = cotangents[0].T
-    grads = [grad]
-    for s in (1, 2, 3):
-        grads.append(send(grad, s))
-    grads = jnp.stack(grads)
 
     owner, row = sample_rows // rows, sample_rows % rows
     slot = (owner >> 3 & 1) * 2 + (owner & 1)
@@ -202,9 +295,8 @@
     odd = odd.reshape(-1, 1, LANES) + odd_bits(lane[None, :, None] & (sample_columns % LANES).reshape(-1, 1, LANES))
     table = (1 - 2 * (odd & 1)).astype(jnp.bfloat16)
 
-    picked = local_call(
-        norm, index, jnp.stack([core, place]), grads, tokens, (sign_flips, z_mine, z_other, x_mine, x_other), table
-    )
+    parcels = (z_mine, z_other, x_mine, x_other)
+    picked = local_call(norm, index, jnp.stack([core, place * span]), tokens, sign_flips, grad, parcels, table)
     return lax.all_to_all(picked.reshape(parts, 1, -1), "param", 0, 0, tiled=True).sum(0)
 
 

time: 118 us -> 130 us (1.10)
  waiting for transfers between devices: 31.4 us -> 47.6 us
  starting transfers between devices: 39 us -> 29.8 us
  Pallas kernels: 13.2 us -> 19.8 us
  local copies, waits for them, and re-layouts: 4.7 us -> 2.39 us
    ppermute x5 -> x2, waiting for transfers between devices: 31.4 us -> 47.6 us  [send(): return lax.ppermute(value, ('param', 'ex'), pairs)]
    ppermute x5 -> x2, starting transfers between devices: 15.6 us -> 6.34 us  [send(): return lax.ppermute(value, ('param', 'ex'), pairs)]
    pallas_call x0 -> x2, Pallas kernels: none -> 6.1 us  [copies_call(): pl.pallas_call(body, out_shape=results, in_specs=[pl.BlockSpec(memory_spa...]
    broadcast_in_dim x1 -> x0, local copies, waits for them, and re-layouts: 2.02 us -> none  [shards(): jnp.broadcast_to(tokens[None, :, None], (ys, xs, zs // 2, 2) + tokens.sha...]
  transfers between devices with their start and end apart: 8 -> 5, of which waited for: 1 -> 2; matrix products, arithmetic and copies ran while one was open for 4% -> 4% of each run, Pallas kernels for 0% -> 2%
where the time goes in v2:
time: 130 us
  waiting for transfers between devices  47.6 us (37%)
  starting transfers between devices  29.8 us (23%)
  blocking collectives  25.8 us (20%)
  Pallas kernels  19.8 us (15%)
  other arithmetic  4.1 us (3%)
  local copies, waits for them, and re-layouts  2.39 us (2%)
    ppermute x2, waiting for transfers between devices, send(): return lax.ppermute(value, ('param', 'ex'), pairs)  47.6 us
    all_to_all x1, blocking collectives, shards(): lax.all_to_all(picked.reshape(parts, 1, -1), 'param', 0, 0, tiled=True)  25.8 us
    all_to_all x1, starting transfers between devices, shards(): lax.all_to_all(spread.reshape(parts, -1, span), 'param', 0, 0, tiled=True)  19.1 us
    pallas_call x1, Pallas kernels, local_call(): pl.pallas_call(functools.partial(kernel, norm), out_shape=jax.ShapeDtypeS...  13.7 us
    ppermute x2, starting transfers between devices, send(): return lax.ppermute(value, ('param', 'ex'), pairs)  6.34 us
    pallas_call x2, Pallas kernels, copies_call(): pl.pallas_call(body, out_shape=results, in_specs=[pl.BlockSpec(memory_spa...  6.1 us
  transfers between devices with their start and end apart: 5, of which 2 were waited for; matrix products, arithmetic and copies ran while one was open for 4% of the time, Pallas kernels for 2%

profile of v2, /device:TPU:4, one launch (start us, length us, event | category | flops | bytes accessed | tf_op | source)
XLA Modules:
  0.0 129.6 jit_solution(4187185050329701061)
XLA Ops:
  0.0 3.3 %shard_map.55 = (bf16[18,128,128]{2,1,0:T(8,128)(2,1)}, bf16[8,2,4,2,2,2048]{5,4,3,2,1,0:T(2,128)(2,1)}) custom-call(s32[1]{0:T(128)} %bitcast.3.start, bf16[2,8192]{1,0:T(2,128)(2,1)} %bitcast.20, bf16[128,8192]{1,0:T(8,128)(2,1)} %own.1, bf16[2,128,128]{2,1,0:T(8,128)(2,1)} %bitcast.15), custom_call_target="tpu_custom_call" | custom-call | tf_op jit(solution)/shard_map/pallas_call | solution.py:195
  3.3 0.0 copy-start.5
  3.3 19.1 %all-to-all-start = ((bf16[128,2,2048]{2,1,0:T(2,128)(2,1)}), bf16[128,2,2048]{2,1,0:T(2,128)(2,1)}, u32[]{:S(2)}, u32[]{:S(2)}) async-start(bf16[128,2,2048]{2,1,0:T(2,128)(2,1)} %bitcast.18), calls=%async_computation | async-start | bytes 2097152 | tf_op jit(solution)/shard_map/all_to_all | solution.py:275
  22.4 0.0 copy-start.3
  22.4 0.0 copy-start.4
  22.5 0.0 copy-done.5
  22.5 3.0 %collective-permute-start = (bf16[18,128,128]{2,1,0:T(8,128)(2,1)S(1)}, bf16[18,128,128]{2,1,0:T(8,128)(2,1)S(1)}, u32[]{:S(2)}, u32[]{:S(2)}) collective-permute-start(bf16[18,128,128]{2,1,0:T(8,128)(2,1)S(1)} %copy-done.5), channel_id=1, source_target_pairs={{0,4},{1,5},{2,6},{3,7},{4,0},{5,1},{6,2},{7,3},{8,12},{9,13},{10,... | collective-permute-start | bytes 1769480 | tf_op jit(solution)/shard_map/ppermute | solution.py:256
  25.4 0.6 pad_add_fusion.1.core
  26.1 32.2 %collective-permute-done.received.z_mine = bf16[18,128,128]{2,1,0:T(8,128)(2,1)S(1)} collective-permute-done((bf16[18,128,128]{2,1,0:T(8,128)(2,1)S(1)}, bf16[18,128,128]{2,1,0:T(8,128)(2,1)S(1)}, u32[]{:S(2)}, u32[]{:S(2)}) %collective-permute-start) | collective-permute-done | bytes 589856 | tf_op jit(solution)/shard_map/ppermute | solution.py:256
  58.3 0.0 copy-start
  58.3 0.8 copy-done
  59.1 2.8 %shard_map.56 = bf16[20,128,128]{2,1,0:T(8,128)(2,1)} custom-call(s32[2]{0:T(128)} %pad_add_fusion.1.core, bf16[128,8192]{1,0:T(8,128)(2,1)} %own.1, bf16[18,128,128]{2,1,0:T(8,128)(2,1)} %copy-done, bf16[2,128,128]{2,1,0:T(8,128)(2,1)} %bitcast.16), custom_call_target="tpu_custom_call" | custom-call | tf_op jit(solution)/shard_map/pallas_call | solution.py:195
  61.9 3.4 %collective-permute-start.2 = (bf16[20,128,128]{2,1,0:T(8,128)(2,1)}, bf16[20,128,128]{2,1,0:T(8,128)(2,1)S(1)}, u32[]{:S(2)}, u32[]{:S(2)}) collective-permute-start(bf16[20,128,128]{2,1,0:T(8,128)(2,1)} %shard_map.56), channel_id=1, source_target_pairs={{0,32},{1,33},{2,34},{3,35},{4,36},{5,37},{6,38},{7,39},{8,40},{9,... | collective-permute-start | bytes 1966088 | tf_op jit(solution)/shard_map/ppermute | solution.py:256
  65.3 15.4 %collective-permute-done.2.x_mine = bf16[20,128,128]{2,1,0:T(8,128)(2,1)S(1)} collective-permute-done((bf16[20,128,128]{2,1,0:T(8,128)(2,1)}, bf16[20,128,128]{2,1,0:T(8,128)(2,1)S(1)}, u32[]{:S(2)}, u32[]{:S(2)}) %collective-permute-start.2) | collective-permute-done | bytes 655392 | tf_op jit(solution)/shard_map/ppermute | solution.py:256
  80.7 1.9 %collective-permute-start.3 = (bf16[20,128,128]{2,1,0:T(8,128)(2,1)S(1)}, bf16[20,128,128]{2,1,0:T(8,128)(2,1)S(1)}, u32[]{:S(2)}, u32[]{:S(2)}) collective-permute-start(bf16[20,128,128]{2,1,0:T(8,128)(2,1)S(1)} %collective-permute-done.2.x_mine), channel_id=1, source_target_pairs={{0,1},{1,0},{2,3},{3,2},{4,5},{5,4},{6,7},{7,6},{8,9},{9,8},{10,11... | collective-permute-start | bytes 1966088 | tf_op jit(solution)/shard_map/ppermute | solution.py:287
  82.6 2.4 %collective-permute-start.1 = (bf16[18,128,128]{2,1,0:T(8,128)(2,1)}, bf16[18,128,128]{2,1,0:T(8,128)(2,1)}, u32[]{:S(2)}, u32[]{:S(2)}) collective-permute-start(bf16[18,128,128]{2,1,0:T(8,128)(2,1)} %copy-done), channel_id=1, source_target_pairs={{0,1},{1,0},{2,3},{3,2},{4,5},{5,4},{6,7},{7,6},{8,9},{9,8},{10,11... | collective-permute-start | bytes 1769480 | tf_op jit(solution)/shard_map/ppermute | solution.py:286
  85.0 0.1 pad_add_fusion.core
  85.1 0.0 copy-done.3
  85.1 0.0 copy-done.4
  85.1 0.1 fusion.10
  85.2 0.0 copy-start.1
  85.2 0.0 copy-start.2
  85.3 2.6 %subtract_convert_fusion.table = bf16[64,128,128]{2,1,0:T(8,128)(2,1)} fusion(s32[64,128]{1,0:T(8,128)S(1)} %get-tuple-element.11, s32[64,128]{1,0:T(8,128)S(1)} %get-tuple-element.9), kind=kLoop, calls=%fused_computation | loop fusion | flops 8388608 | bytes 2162688 | tf_op jit(solution)/shard_map/convert_element_type | solution.py:296
  87.8 0.0 all-to-all-done
  87.8 1.5 %reshape.19.tokens = bf16[256,2048]{1,0:T(8,128)(2,1)S(1)} reshape(bf16[128,2,2048]{2,1,0:T(2,128)(2,1)} %all-to-all-done) | data formatting | bytes 2097152 | tf_op jit(solution)/shard_map/reshape | solution.py:276
  89.3 0.0 collective-permute-done.1.z_other
  89.3 0.0 collective-permute-done.3.x_other
  89.3 0.0 copy-done.1
  89.3 0.0 copy-done.2
  89.4 13.7 %shard_map.57 = f32[64,128]{1,0:T(8,128)S(1)} custom-call(s32[64,128]{1,0:T(8,128)S(1)} %get-tuple-element.10.index, s32[2]{0:T(128)S(1)} %pad_add_fusion.core, bf16[256,2048]{1,0:T(8,128)(2,1)S(1)} %reshape.19.tokens, bf16[128,8192]{1,0:T(8,128)(2,1)} %own.1, bf16[2,128,128]{2,1,0:T(8,128)(2,1)S(1)} %bitcast.17, bf16[18,128,128]{2,1,0:T(8,128)(2,1)S(1)} %copy-done.1, ...), custom_call_target="tpu_custom_call" | custom-call | tf_op jit(solution)/shard_map/pallas_call | solution.py:210
  103.1 0.1 reshape.20
  103.2 25.8 %all_to_all.10 = f32[128,1,64]{2,1,0:T(1,128)S(1)} all-to-all(f32[128,1,64]{2,1,0:T(1,128)S(1)} %bitcast.19), channel_id=1, replica_groups=mesh['param'=128,'ex'=4] {'param'}, dimensions={0} | all-to-all | bytes 65536 | tf_op jit(solution)/shard_map/all_to_all | solution.py:300
  129.0 0.7 reduce_sum.11
  (2 shorter events, 0.0 us)
Async XLA Ops:
  3.3 19.2 %copy-start.5 = (bf16[18,128,128]{2,1,0:T(8,128)(2,1)S(1)}, bf16[18,128,128]{2,1,0:T(8,128)(2,1)}, u32[]{:S(2)}) copy-start(bf16[18,128,128]{2,1,0:T(8,128)(2,1)} %get-tuple-element.8) | copy-start | bytes 1769476
  3.3 84.5 %all-to-all-start = ((bf16[128,2,2048]{2,1,0:T(2,128)(2,1)}), bf16[128,2,2048]{2,1,0:T(2,128)(2,1)}, u32[]{:S(2)}, u32[]{:S(2)}) async-start(bf16[128,2,2048]{2,1,0:T(2,128)(2,1)} %bitcast.18), calls=%async_computation | async-start | bytes 2097152 | tf_op jit(solution)/shard_map/all_to_all | solution.py:275
  22.4 62.7 %copy-start.3 = (s32[8192]{0:T(1024)S(1)}, s32[8192]{0:T(1024)}, u32[]{:S(2)}) copy-start(s32[8192]{0:T(1024)} %param.9) | copy-start | bytes 98308
  22.4 62.7 %copy-start.4 = (s32[8192]{0:T(1024)S(1)}, s32[8192]{0:T(1024)}, u32[]{:S(2)}) copy-start(s32[8192]{0:T(1024)} %param.8) | copy-start | bytes 98308
  22.5 35.8 %collective-permute-start = (bf16[18,128,128]{2,1,0:T(8,128)(2,1)S(1)}, bf16[18,128,128]{2,1,0:T(8,128)(2,1)S(1)}, u32[]{:S(2)}, u32[]{:S(2)}) collective-permute-start(bf16[18,128,128]{2,1,0:T(8,128)(2,1)S(1)} %copy-done.5), channel_id=1, source_target_pairs={{0,4},{1,5},{2,6},{3,7},{4,0},{5,1},{6,2},{7,3},{8,12},{9,13},{10,... | collective-permute-start | bytes 1769480 | tf_op jit(solution)/shard_map/ppermute | solution.py:256
  58.3 0.8 copy-start
  61.9 18.8 %collective-permute-start.2 = (bf16[20,128,128]{2,1,0:T(8,128)(2,1)}, bf16[20,128,128]{2,1,0:T(8,128)(2,1)S(1)}, u32[]{:S(2)}, u32[]{:S(2)}) collective-permute-start(bf16[20,128,128]{2,1,0:T(8,128)(2,1)} %shard_map.56), channel_id=1, source_target_pairs={{0,32},{1,33},{2,34},{3,35},{4,36},{5,37},{6,38},{7,39},{8,40},{9,... | collective-permute-start | bytes 1966088 | tf_op jit(solution)/shard_map/ppermute | solution.py:256
  80.7 8.6 %collective-permute-start.3 = (bf16[20,128,128]{2,1,0:T(8,128)(2,1)S(1)}, bf16[20,128,128]{2,1,0:T(8,128)(2,1)S(1)}, u32[]{:S(2)}, u32[]{:S(2)}) collective-permute-start(bf16[20,128,128]{2,1,0:T(8,128)(2,1)S(1)} %collective-permute-done.2.x_mine), channel_id=1, source_target_pairs={{0,1},{1,0},{2,3},{3,2},{4,5},{5,4},{6,7},{7,6},{8,9},{9,8},{10,11... | collective-permute-start | bytes 1966088 | tf_op jit(solution)/shard_map/ppermute | solution.py:287
  82.6 6.7 %collective-permute-start.1 = (bf16[18,128,128]{2,1,0:T(8,128)(2,1)}, bf16[18,128,128]{2,1,0:T(8,128)(2,1)}, u32[]{:S(2)}, u32[]{:S(2)}) collective-permute-start(bf16[18,128,128]{2,1,0:T(8,128)(2,1)} %copy-done), channel_id=1, source_target_pairs={{0,1},{1,0},{2,3},{3,2},{4,5},{5,4},{6,7},{7,6},{8,9},{9,8},{10,11... | collective-permute-start | bytes 1769480 | tf_op jit(solution)/shard_map/ppermute | solution.py:286
  85.2 4.1 %copy-start.1 = (bf16[18,128,128]{2,1,0:T(8,128)(2,1)S(1)}, bf16[18,128,128]{2,1,0:T(8,128)(2,1)}, u32[]{:S(2)}) copy-start(bf16[18,128,128]{2,1,0:T(8,128)(2,1)} %copy-done) | copy-start | bytes 1769476
  85.2 4.1 %copy-start.2 = (bf16[1,256,128]{2,1,0:T(8,128)(2,1)S(1)}, bf16[1,256,128]{2,1,0:T(8,128)(2,1)}, u32[]{:S(2)}) copy-start(bf16[1,256,128]{2,1,0:T(8,128)(2,1)} %param.6) | copy-start | bytes 196612
